TPU v7x, 512 devices: a whole 4x8x8 slice. The times are simulated.
512 devices in a mesh: ep: 128 (over z, y, core), tp: 4 (over x).
Axes of the slice: x: 4, y: 8, z: 8, core: 2. Of those that a mesh axis runs over, the one named last changes fastest.
Arguments:
- grad_out: bfloat16 [16384, 3584], P('ep', 'tp'), may hold values from -6 to 6
- routes: int32 [16384, 8], P('ep'), may hold values from 0 to 127, all different within a row; in each aligned block of 128 rows (0 to 127, 128 to 255, ...) at most 10 rows name the same one
- gate_weights: float32 [16384, 8], P('ep'), may hold values from 0.05 to 0.5
- gate_act: bfloat16 [128, 1280, 1024], P('ep', None, 'tp'), may hold values from -6 to 6
- w_down: bfloat16 [128, 1024, 3584], P('ep', None, 'tp'), may hold values from -0.1875 to 0.1875
- w_up: bfloat16 [128, 3584, 1024], P('ep', 'tp'), may hold values from -0.09375 to 0.09375
Outputs:
- grad_in: bfloat16 [16384, 3584], P('ep', 'tp')
Inputs may be any that keep to these rules, and one draw needn't show every extreme that they name: `routes`: each row names 8 different experts; among the 128 rows of one device no expert is named more than 10 times, a bound that some block reaches.
All inputs are finite; a program needn't handle non-finite values.
Results may differ from a plain program's by a relative error of at most 0.02.
Values may be sent and summed in bfloat16 or wider, within the bound.
A program may use at most 64 MiB of HBM per device.

v0:
```python
import jax
import jax.numpy as jnp
from jax import lax
from jax.sharding import PartitionSpec as P


def on_device(grad_out, routes, gate_weights, gate_act, w_down, w_up):
    experts_n = lax.axis_size("ep")
    slot_n = gate_act.shape[1] // experts_n
    rows_n = experts_n * slot_n
    token_n, choose_n = routes.shape
    flat_ids = routes.reshape(-1)
    one_hot = (flat_ids[:, None] == jnp.arange(experts_n, dtype=jnp.int32)[None, :]).astype(
        jnp.int32
    )
    earlier = jnp.cumsum(one_hot, axis=0) - one_hot
    slot_rank = jnp.sum(earlier * one_hot, axis=1)
    position = flat_ids * slot_n + slot_rank
    token_ids = jnp.arange(token_n * choose_n, dtype=jnp.int32) // choose_n
    token_of = jnp.full((rows_n,), token_n, jnp.int32).at[position].set(token_ids)
    weight_of = jnp.zeros((rows_n,), jnp.float32).at[position].set(gate_weights.reshape(-1))
    down_local = w_down[0]
    up_local = w_up[0]
    feat_part = grad_out.shape[1]
    padded = jnp.concatenate([grad_out, jnp.zeros((1, feat_part), grad_out.dtype)], axis=0)
    placed = (padded[token_of].astype(jnp.float32) * weight_of[:, None]).astype(jnp.bfloat16)
    placed = placed.reshape(experts_n, slot_n, feat_part)
    partial_value = jnp.einsum(
        "nsd,fd->nsf",
        lax.all_to_all(placed, "ep", split_axis=0, concat_axis=0, tiled=True),
        down_local,
        preferred_element_type=jnp.float32,
    )
    partial_value = partial_value.reshape(rows_n, -1)
    hidden_grad = lax.psum_scatter(
        partial_value.astype(jnp.bfloat16), "tp", scatter_dimension=1, tiled=True
    ).astype(jnp.float32)
    up_grad = (hidden_grad * gate_act[0].astype(jnp.float32)).astype(jnp.bfloat16)
    row_grad = lax.dot_general(
        lax.all_gather(up_grad, "tp", axis=1, tiled=True),
        up_local,
        (((1,), (1,)), ((), ())),
        preferred_element_type=jnp.float32,
    )
    row_grad = row_grad.astype(jnp.bfloat16).reshape(experts_n, slot_n, -1)
    returned = lax.all_to_all(row_grad, "ep", split_axis=0, concat_axis=0, tiled=True)
    picked = returned.reshape(rows_n, -1)[position]
    summed = jnp.sum(picked.astype(jnp.float32).reshape(token_n, choose_n, -1), axis=1)
    return summed.astype(jnp.bfloat16)


def solution(mesh):
    placed = (
        P("ep", "tp"),
        P("ep", None),
        P("ep", None),
        P("ep", None, "tp"),
        P("ep", None, "tp"),
        P("ep", "tp", None),
    )
    return jax.shard_map(
        on_device, mesh=mesh, in_specs=placed, out_specs=P("ep", "tp"), check_vma=False
    )
```

profile of v0, /device:TPU:6, one launch (start us, length us, event | category | flops | bytes accessed | tf_op | source)
XLA Modules:
  0.0 367.8 jit_solution(9736080060847365617)
XLA Ops:
  6.5 0.0 copy-start
  6.5 0.0 copy-start.2
  6.5 0.0 reduce-scatter.2.cloned.1.call-start
  6.5 0.8 broadcast_multiply_fusion
  7.4 0.8 copy.8
  8.2 0.1 eq.29
  8.3 0.1 eq.25
  8.4 0.1 copy.7
  8.5 0.1 mul.35
  8.6 0.1 copy.10
  8.7 0.8 copy.12
  9.5 0.1 reshape.105
  9.5 0.2 fusion.5
  9.8 0.1 copy.11
  10.0 0.4 fusion.4
  10.3 4.3 %scatter_custom_fusion = s32[1280]{0:T(1024)S(1)} fusion(s32[1024]{0:T(1024)S(1)} %bitcast.28, s32[1024]{0:T(1024)S(1)} %add_select_fusion, s32[]{:T(128)} %constant.29.clone.1), kind=kCustom, calls=%fused_computation.33 | custom fusion | bytes 5124 | tf_op jit(solution)/shard_map/scatter | solution.py:20
  14.7 4.3 %scatter_custom_fusion.1 = f32[1280]{0:T(1024)S(1)} fusion(s32[1024]{0:T(1024)S(1)} %bitcast.29, f32[1024]{0:T(1024)S(1)} %reshape.105, f32[]{:T(128)} %constant.38.clone.1), kind=kCustom, calls=%fused_computation.31 | custom fusion | bytes 5124 | tf_op jit(solution)/shard_map/scatter | solution.py:21
  19.0 0.1 mul.37
  19.1 0.0 copy-done.2
  19.2 5.0 %gather_fusion = bf16[1280,896]{1,0:T(8,128)(2,1)} fusion(bf16[129,896]{1,0:T(8,128)(2,1)S(1)} %concatenate.3, s32[2048]{0:T(1024)S(1)} %pad_clamp_fusion), kind=kCustom, calls=%fused_computation | custom fusion | bytes 4592640 | tf_op jit(solution)/shard_map/gather | solution.py:26
  24.2 5.6 %reshape.75 = f32[128,10,896]{2,1,0:T(8,128)} reshape(bf16[1280,896]{1,0:T(8,128)(2,1)} %gather_fusion) | data formatting | bytes 6881280 | tf_op jit(solution)/shard_map/convert_element_type | solution.py:26
  29.8 3.6 multiply_convert_fusion
  33.4 102.3 %all_to_all.10 = bf16[128,10,896]{2,1,0:T(8,128)(2,1)} all-to-all(bf16[128,10,896]{2,1,0:T(8,128)(2,1)S(1)} %multiply_convert_fusion), channel_id=1, replica_groups=mesh['ep'=128,'tp'=4] {'ep'}, dimensions={0} | all-to-all | bytes 4587520 | tf_op jit(solution)/shard_map/all_to_all | solution.py:30
  135.7 5.3 %dot_general.8 = bf16[1280,896]{1,0:T(8,128)(2,1)} reshape(bf16[128,10,896]{2,1,0:T(8,128)(2,1)} %all_to_all.10) | data formatting | bytes 4587520 | tf_op jit(solution)/shard_map/nsd,fd->nsf/dot_general | solution.py:28
  141.0 0.0 copy-done
  141.0 5.9 %convolution_convert_fusion = bf16[1280,1024]{1,0:T(8,128)(2,1)} fusion(bf16[1280,896]{1,0:T(8,128)(2,1)} %dot_general.8, bf16[1,1024,896]{2,1,0:T(8,128)(2,1)S(1)} %copy-done), kind=kOutput, calls=%fused_computation.5 | convolution fusion | flops 2350120960 | bytes 6750208 | tf_op jit(solution)/shard_map/nsd,fd->nsf/dot_general | solution.py:28
  147.0 0.0 copy-start.1
  147.0 0.0 reduce-scatter.2.cloned.1.call-update
  147.0 0.0 all-gather.2.cloned.1.call-start
  147.1 38.9 %reduce-scatter.2.cloned.1.call-done = bf16[1280,256]{1,0:T(8,128)(2,1)} async-done(((bf16[1280,1024]{1,0:T(8,128)(2,1)}), bf16[1280,256]{1,0:T(8,128)(2,1)}) %reduce-scatter.2.cloned.1.call-update) | async-done | bytes 655376 | tf_op jit(solution)/shard_map/reduce_scatter | solution.py:35
  186.0 0.0 copy-done.1
  186.0 2.1 fusion.2
  188.1 0.0 all-gather.2.cloned.1.call-update
  188.1 45.3 %all-gather.2.cloned.1.call-done = bf16[1280,1024]{1,0:T(8,128)(2,1)} async-done(((bf16[1280,256]{1,0:T(8,128)(2,1)}), bf16[1280,1024]{1,0:T(8,128)(2,1)}) %all-gather.2.cloned.1.call-update) | async-done | bytes 2621456 | tf_op jit(solution)/shard_map/all_gather | solution.py:40
  233.4 6.7 %convolution_convert_fusion.1 = bf16[1280,896]{1,0:T(8,128)(2,1)} fusion(bf16[1280,1024]{1,0:T(8,128)(2,1)} %all-gather.2.cloned.1.call-done, bf16[1,896,1024]{2,1,0:T(8,128)(2,1)} %param.11), kind=kOutput, calls=%fused_computation.6 | convolution fusion | flops 2349957120 | bytes 6750208 | tf_op jit(solution)/shard_map/dot_general | solution.py:39
  240.1 5.2 %reshape.73 = bf16[128,10,896]{2,1,0:T(8,128)(2,1)} reshape(bf16[1280,896]{1,0:T(8,128)(2,1)} %convolution_convert_fusion.1) | data formatting | bytes 4587520 | tf_op jit(solution)/shard_map/reshape | solution.py:45
  245.3 15.0 %all-to-all-start.1 = ((bf16[128,10,896]{2,1,0:T(8,128)(2,1)}), bf16[128,10,896]{2,1,0:T(8,128)(2,1)}, u32[]{:S(2)}, u32[]{:S(2)}) async-start(bf16[128,10,896]{2,1,0:T(8,128)(2,1)} %reshape.73), calls=%async_computation.2 | async-start | bytes 7340032 | tf_op jit(solution)/shard_map/all_to_all | solution.py:46
  260.3 84.3 %all-to-all-done.1 = bf16[128,10,896]{2,1,0:T(8,128)(2,1)} async-done(((bf16[128,10,896]{2,1,0:T(8,128)(2,1)}), bf16[128,10,896]{2,1,0:T(8,128)(2,1)}, u32[]{:S(2)}, u32[]{:S(2)}) %all-to-all-start.1) | async-done | bytes 2293792 | tf_op jit(solution)/shard_map/all_to_all | solution.py:46
  344.5 5.3 %reshape.74 = bf16[1280,896]{1,0:T(8,128)(2,1)} reshape(bf16[128,10,896]{2,1,0:T(8,128)(2,1)} %all-to-all-done.1) | data formatting | bytes 4587520 | tf_op jit(solution)/shard_map/reshape | solution.py:47
  349.9 7.7 %gather_fusion.1 = bf16[1024,896]{1,0:T(8,128)(2,1)} fusion(bf16[1280,896]{1,0:T(8,128)(2,1)} %reshape.74, s32[1024]{0:T(1024)S(1)} %broadcast_clamp_fusion), kind=kCustom, calls=%fused_computation.1 | custom fusion | bytes 3674112 | tf_op jit(solution)/shard_map/gather | solution.py:47
  357.5 3.4 bitcast_reduce_fusion
  (10 shorter events, 0.1 us)
Async XLA Ops:
  6.5 134.5 %copy-start = (bf16[1,1024,896]{2,1,0:T(8,128)(2,1)S(1)}, bf16[1,1024,896]{2,1,0:T(8,128)(2,1)}, u32[]{:S(2)}) copy-start(bf16[1,1024,896]{2,1,0:T(8,128)(2,1)} %param.10) | copy-start | bytes 5505028
  6.5 12.6 %copy-start.2 = (bf16[128,896]{1,0:T(8,128)(2,1)S(1)}, bf16[128,896]{1,0:T(8,128)(2,1)}, u32[]{:S(2)}) copy-start(bf16[128,896]{1,0:T(8,128)(2,1)} %param.6) | copy-start | bytes 688132
  6.5 179.5 %reduce-scatter.2.cloned.1.call-start = ((), (), s32[]{:S(2)}) async-start(), calls=%async_computation.3 | async-start | bytes 3276800 | tf_op jit(solution)/shard_map/reduce_scatter | solution.py:35
  147.0 39.0 %copy-start.1 = (bf16[1,1280,256]{2,1,0:T(8,128)(2,1)S(1)}, bf16[1,1280,256]{2,1,0:T(8,128)(2,1)}, u32[]{:S(2)}) copy-start(bf16[1,1280,256]{2,1,0:T(8,128)(2,1)} %param.9) | copy-start | bytes 1966084
  147.0 86.4 %all-gather.2.cloned.1.call-start = ((), (), s32[]{:S(2)}) async-start(), calls=%async_computation.4 | async-start | bytes 3276800 | tf_op jit(solution)/shard_map/all_gather | solution.py:40
  245.3 99.3 %all-to-all-start.1 = ((bf16[128,10,896]{2,1,0:T(8,128)(2,1)}), bf16[128,10,896]{2,1,0:T(8,128)(2,1)}, u32[]{:S(2)}, u32[]{:S(2)}) async-start(bf16[128,10,896]{2,1,0:T(8,128)(2,1)} %reshape.73), calls=%async_computation.2 | async-start | bytes 7340032 | tf_op jit(solution)/shard_map/all_to_all | solution.py:46
Sparse Core Ops, SparseCore 0:
  147.1 38.8 reduce-scatter.1
  188.2 45.1 all-gather.1
where the time goes:
time: 372 us; the launch traced here: 368 us
  waiting for transfers between devices  169 us (45%)
  blocking collectives  102 us (27%)
  local copies, waits for them, and re-layouts  45.2 us (12%)
  starting transfers between devices  15 us (4%)
  between operations  13.5 us (4%)
  matrix products  12.6 us (3%)
  other arithmetic  10.6 us (3%)
    all_to_all x1, blocking collectives, on_device(): lax.all_to_all(placed, 'ep', split_axis=0, concat_axis=0, tiled=True)  102 us
    all_to_all x1, waiting for transfers between devices, on_device(): lax.all_to_all(row_grad, 'ep', split_axis=0, concat_axis=0, tiled=True)  84.3 us
    all_gather x1, waiting for transfers between devices, on_device(): lax.all_gather(up_grad, 'tp', axis=1, tiled=True)  45.3 us
    reduce_scatter x1, waiting for transfers between devices, on_device(): lax.psum_scatter(partial_value.astype(jnp.bfloat16), 'tp', scatter_dimens...  38.9 us
    all_to_all x1, starting transfers between devices, on_device(): lax.all_to_all(row_grad, 'ep', split_axis=0, concat_axis=0, tiled=True)  15 us
    gather x1, local copies, waits for them, and re-layouts, on_device(): picked = returned.reshape(rows_n, -1)[position]  7.67 us
  transfers between devices with their start and end apart: 3, of which 3 were waited for; matrix products, arithmetic and copies ran while one was open for 0% of the time, Pallas kernels for 0%

commit v1 on v0

v1 whole, which is shorter than its diff:
```python
import functools

import jax
import jax.numpy as jnp
from jax import lax
from jax.experimental import pallas as pl
from jax.experimental.pallas import tpu as pltpu
from jax.sharding import PartitionSpec as P

MESH = pl.DeviceIdType.MESH
RING = 8
SLOT = 10
CHUNKS = 8
FIRST = 3
NEAR = (0, 1, 7, 2, 6, 3, 5, 4)
PLACE = {offset: place for place, offset in enumerate(NEAR)}
GATHER_AHEAD = 3
COMBINE_LAG = 6
BF16 = jnp.bfloat16
F32 = jnp.float32
ABT = (((1,), (1,)), ((), ()))
ATB = (((0,), (0,)), ((), ()))


def hop_of(chunk):
    return lax.rem(chunk * 3 + FIRST, RING)


def on_core(
    grad_ref, ids_ref, gates_ref, act_hbm, down_hbm, up_hbm, out_ref,
    act, down, up, act_rows, meta_out, meta, tokens, picks, to_expert, routed,
    hidden, relay, passed, arrived, wide, row_grad, returned, totals, sum_out, sum_in,
    load_sem, a_send, a_recv, m_send, m_recv, b_send, b_recv, r_send, r_recv,
    p_send, p_recv, g_send, g_recv, f_send, f_recv, y_send, y_recv, s_send, s_recv,
):
    token_n, feat = grad_ref.shape
    half_tok = token_n // 2
    msg = RING * SLOT
    ep, tp = lax.axis_index("ep"), lax.axis_index("tp")
    tp_n = lax.axis_size("tp")
    core = lax.rem(ep, 2)
    y = lax.rem(ep // 2, RING)
    z = ep // (2 * RING)
    a = z * (1 - core) + y * core
    b = y * (1 - core) + z * core

    def device(a_at, b_at, role, core_at):
        return (a_at * (RING - (RING - 1) * role) + b_at * (1 + (RING - 1) * role)) * 2 + core_at

    def ring(value):
        return lax.rem(value + 2 * RING, RING)

    right, left = lax.rem(tp + 1, tp_n), lax.rem(tp + tp_n - 1, tp_n)
    across = lax.rem(tp + 2, tp_n)

    barrier = pltpu.get_barrier_semaphore()
    for other in range(2):
        for step in range(RING):
            for z_at, y_at in ((ring(z + step), y), (z, ring(y + step)))[: 1 if step == 0 else 2]:
                peer = (z_at * RING + y_at) * 2 + lax.rem(core + other, 2)
                if step or other:
                    pl.semaphore_signal(barrier, inc=1, device_id=(peer, tp), device_id_type=MESH)
    for peer in (right, left):
        pl.semaphore_signal(barrier, inc=1, device_id=(ep, peer), device_id_type=MESH)

    loads = [
        pltpu.make_async_copy(src, dst, load_sem.at[i])
        for i, (src, dst) in enumerate(((act_hbm, act), (down_hbm, down), (up_hbm, up)))
    ]
    for load in loads:
        load.start()

    def remote(src, dst, send, recv, to):
        return pltpu.make_async_remote_copy(
            src_ref=src, dst_ref=dst, send_sem=send, recv_sem=recv, device_id=to, device_id_type=MESH
        )

    def arrival(ref, sem):
        pltpu.make_async_copy(ref, ref, sem).wait()

    shape = (token_n, token_n)
    row = lax.broadcasted_iota(jnp.int32, shape, 0)
    chunk_of, core_of = (row >> 1) & 7, row & 1
    a_of = (row // 16 + a) & 7
    b_of = (chunk_of * 3 + FIRST + b) & 7
    expert = a_of * (16 - 14 * core) + b_of * (2 + 14 * core) + core_of
    named = jnp.zeros(shape, F32)
    weight = jnp.zeros(shape, F32)
    for k in range(ids_ref.shape[0]):
        hit = expert == ids_ref[k : k + 1, :]
        named = jnp.where(hit, 1.0, named)
        weight = jnp.where(hit, gates_ref[k : k + 1, :], weight)
    before = (row < lax.broadcasted_iota(jnp.int32, shape, 1)).astype(BF16)
    rank = jnp.dot(named.astype(BF16), before, preferred_element_type=F32)
    slot = jnp.where(named > 0.0, rank, -1000.0)
    for m in range(RING):
        meta_out[m, 0:16, :] = slot[m * 16 : (m + 1) * 16, :]
        meta_out[m, 16:32, :] = weight[m * 16 : (m + 1) * 16, :]
    meta[0] = meta_out[0]
    tokens[0] = grad_ref[...]
    totals[...] = jnp.zeros(totals.shape, F32)

    pl.semaphore_wait(barrier, 4 * (RING - 1) + 1 + 2)

    steps_of = ((4, 3), (3, 4))
    a_next = (device(ring(a + 1), b, core, core), device(ring(a - 1), b, core, core))

    def spread(way, h, s):
        rows = pl.ds(h * half_tok, half_tok)
        src_off, dst_off = ((RING - s) % RING, RING - 1 - s) if way == 0 else (s, s + 1)
        src = grad_ref.at[rows] if s == 0 else tokens.at[PLACE[src_off], rows]
        at = (way * 2 + h) * 4 + s
        return remote(
            src, tokens.at[PLACE[dst_off], rows], a_send.at[at], a_recv.at[at], (a_next[way], tp)
        )

    metas = [
        remote(
            meta_out.at[m], meta.at[PLACE[RING - m]], m_send.at[m], m_recv.at[RING - m],
            (device(ring(a + m), b, core, core), tp),
        )
        for m in range(1, RING)
    ]
    for copy in metas:
        copy.start()

    act_n = act.shape[0]
    wide_shape = (2 * msg, 128)
    row = lax.broadcasted_iota(jnp.int32, wide_shape, 0)
    lane = lax.broadcasted_iota(jnp.int32, wide_shape, 1)
    from_one = row >= msg
    inner = jnp.where(from_one, row - msg, row)
    offset = jnp.full(wide_shape, NEAR[0], jnp.int32)
    in_slot = inner
    for place in range(1, RING):
        past = inner >= place * SLOT
        offset = jnp.where(past, NEAR[place], offset)
        in_slot = jnp.where(past, inner - place * SLOT, in_slot)
    act_base = in_slot + jnp.where(
        from_one,
        ((offset + y) & 7) * (2 * SLOT) + SLOT,
        ((offset + z) & 7) * (2 * SLOT * RING),
    )

    def order_act(k, carry):
        hop = hop_of(k)
        natural = act_base + jnp.where(
            from_one, ring(z - hop) * (2 * SLOT * RING), ring(y - hop) * (2 * SLOT)
        )
        pick = jnp.concatenate(
            [(lane + i * 128 == natural).astype(F32).astype(BF16) for i in range(act_n // 128)], axis=1
        )
        got = jnp.dot(pick, act[...], preferred_element_type=F32).astype(BF16)
        act_rows[k] = got.reshape(act_rows.shape[1:])
        return carry

    for s in range(4):
        for h in range(2):
            for way in range(2):
                if s < steps_of[way][h]:
                    if s:
                        spread(way, h, s - 1).wait_recv()
                    spread(way, h, s).start()
        if s == 0:
            loads[0].wait()
        lax.fori_loop(s * 2, s * 2 + 2, order_act, 0)
    for way in range(2):
        for h in range(2):
            spread(way, h, steps_of[way][h] - 1).wait_recv()
    for m in range(1, RING):
        metas[m - 1].wait_recv()
    loads[1].wait()
    loads[2].wait()

    msg_row = lax.broadcasted_iota(jnp.int32, (msg, token_n), 0).astype(F32)

    def gather(k):
        hop = hop_of(k)
        gates = []
        for c in range(2):
            gate = jnp.zeros((msg, token_n), F32)
            for place in range(RING):
                at = meta[place, pl.ds(k * 2 + c, 1), :] + float(place * SLOT)
                hit = msg_row == at
                gate = jnp.where(hit, meta[place, pl.ds(16 + k * 2 + c, 1), :], gate)
                picks[k, c * msg : (c + 1) * msg, place * token_n : (place + 1) * token_n] = (
                    jnp.where(hit, 1.0, 0.0).astype(BF16)
                )
            gates.append(jnp.sum(gate, axis=1, keepdims=True))
        rows = jnp.dot(
            picks[k], tokens[...].reshape(RING * token_n, feat), preferred_element_type=F32
        )
        for c in range(2):
            to_expert[k, c] = (rows[c * msg : (c + 1) * msg] * gates[c]).astype(BF16)
        for c in range(2):
            here = jnp.logical_and(hop == 0, core == c)

            @pl.when(here)
            def _():
                pltpu.make_async_copy(to_expert.at[k, c], routed.at[k, core], b_recv.at[k, core]).start()

            @pl.when(jnp.logical_not(here))
            def _():
                remote(
                    to_expert.at[k, c], routed.at[k, core], b_send.at[k, c], b_recv.at[k, core],
                    (device(a, ring(b + hop), core, c), tp),
                ).start()

    def r_copy(k, i):
        src, dst, to = (
            (hidden.at[k, across, 0], relay.at[k, 0], right),
            (hidden.at[k, right, 1], arrived.at[k, 0, 1], right),
            (hidden.at[k, across, 1], relay.at[k, 1], left),
            (hidden.at[k, left, 0], arrived.at[k, 1, 0], left),
        )[i]
        return remote(src, dst, r_send.at[k, i], r_recv.at[k, i], (ep, to))

    def p_copy(k, way):
        dst, to = ((arrived.at[k, 0, 0], right), (arrived.at[k, 1, 1], left))[way]
        return remote(passed.at[k, way], dst, p_send.at[k, way], p_recv.at[k, way], (ep, to))

    def g_copy(k, way):
        return remote(
            wide.at[k, tp], wide.at[k, tp], g_send.at[k, way], g_recv.at[k, way],
            (ep, (right, left)[way]),
        )

    def f_copy(k, way):
        part = wide.at[k, (left, right)[way], way]
        return remote(part, part, f_send.at[k, way], f_recv.at[k, way], (ep, (right, left)[way]))

    def project_down(k):
        for c in range(2):
            arrival(routed.at[k, c], b_recv.at[k, c])
        rows = routed[k].reshape(2 * msg, feat)
        part = hidden.shape[-1]
        for q in range(hidden.shape[1]):
            value = lax.dot_general(
                rows, down[q * part : (q + 1) * part, :], ABT, preferred_element_type=F32
            )
            hidden[k, q] = value.astype(BF16).reshape(2, msg, part)
        for i in (0, 2, 1, 3):
            r_copy(k, i).start()

    def pass_on(k):
        for way, to in ((0, right), (1, left)):
            r_copy(k, way * 2).wait_recv()
            passed[k, way] = (
                hidden[k, to, way].astype(F32) + relay[k, way].astype(F32)
            ).astype(BF16)
            p_copy(k, way).start()

    def finish_hidden(k):
        r_copy(k, 1).wait_recv()
        r_copy(k, 3).wait_recv()
        p_copy(k, 0).wait_recv()
        p_copy(k, 1).wait_recv()
        value = hidden[k, tp].astype(F32) + (
            arrived[k, 0].astype(F32) + arrived[k, 1].astype(F32)
        )
        wide[k, tp] = (value * act_rows[k].astype(F32)).astype(BF16)
        for way in range(2):
            g_copy(k, way).start()

    def hand_over(k):
        for way in range(2):
            arrival(wide.at[k, (left, right)[way]], g_recv.at[k, way])
            f_copy(k, way).start()

    def project_up(k):
        for way in range(2):
            arrival(wide.at[k, across, way], f_recv.at[k, way])
        part = wide.shape[-1]
        rows = jnp.concatenate(
            [wide[k, q].reshape(2 * msg, part) for q in range(wide.shape[1])], axis=1
        )
        value = lax.dot_general(rows, up[...], ABT, preferred_element_type=F32).astype(BF16)
        row_grad[k] = value.reshape(2, msg, feat)
        hop = hop_of(k)
        for c in range(2):
            here = jnp.logical_and(hop == 0, core == c)
            to = device(z, ring(y - hop), 0, 0) if c == 0 else device(y, ring(z - hop), 1, 1)

            @pl.when(here)
            def _():
                pltpu.make_async_copy(row_grad.at[k, c], returned.at[k, core], y_recv.at[k, core]).start()

            @pl.when(jnp.logical_not(here))
            def _():
                remote(
                    row_grad.at[k, c], returned.at[k, core], y_send.at[k, c], y_recv.at[k, core],
                    (to, tp),
                ).start()

    def combine(k):
        for c in range(2):
            arrival(returned.at[k, c], y_recv.at[k, c])
        rows = returned[k].reshape(2 * msg, feat)
        value = lax.dot_general(picks[k], rows, ATB, preferred_element_type=F32)
        totals[...] += value.reshape(totals.shape)

    def first(k, carry):
        gather(k)
        return carry

    lax.fori_loop(0, GATHER_AHEAD, first, 0)

    stages = (
        (project_down, 0),
        (pass_on, 1),
        (finish_hidden, 2),
        (hand_over, 3),
        (project_up, 4),
        (combine, COMBINE_LAG),
    )

    def turn(t, carry):
        for stage, lag in stages:

            @pl.when(jnp.logical_and(t >= lag, t < lag + CHUNKS))
            def _():
                stage(t - lag)

            if lag == 0:

                @pl.when(t < CHUNKS - GATHER_AHEAD)
                def _():
                    gather(t + GATHER_AHEAD)

        return carry

    lax.fori_loop(0, CHUNKS + COMBINE_LAG, turn, 0)

    chain_of = (((4, 3, 2, 1), (3, 2, 1)), ((5, 6, 7), (4, 5, 6, 7)))

    def sum_copy(way, h, s):
        at = (way * 2 + h) * 4 + s
        return remote(
            sum_out.at[way, h, s], sum_in.at[way, h, s], s_send.at[at], s_recv.at[at],
            (a_next[way], tp),
        )

    for s in range(4):
        for h, way in ((0, 0), (1, 1), (1, 0), (0, 1)):
            chain = chain_of[way][h]
            if s < len(chain):
                value = totals[PLACE[chain[s]], h * half_tok : (h + 1) * half_tok, :]
                if s:
                    sum_copy(way, h, s - 1).wait_recv()
                    value = value + sum_in[way, h, s - 1].astype(F32)
                sum_out[way, h, s] = value.astype(BF16)
                sum_copy(way, h, s).start()
    for h in range(2):
        value = totals[0, h * half_tok : (h + 1) * half_tok, :]
        for way in range(2):
            last = len(chain_of[way][h]) - 1
            sum_copy(way, h, last).wait_recv()
            value = value + sum_in[way, h, last].astype(F32)
        out_ref[h * half_tok : (h + 1) * half_tok, :] = value.astype(BF16)

    for copy in metas:
        copy.wait_send()
    for way in range(2):
        for h in range(2):
            for s in range(steps_of[way][h]):
                spread(way, h, s).wait_send()
                sum_copy(way, h, s).wait_send()

    def drain(k, carry):
        hop = hop_of(k)
        for c in range(2):

            @pl.when(jnp.logical_not(jnp.logical_and(hop == 0, core == c)))
            def _():
                arrival(to_expert.at[k, c], b_send.at[k, c])
                arrival(row_grad.at[k, c], y_send.at[k, c])

        for i in range(4):
            r_copy(k, i).wait_send()
        for way in range(2):
            p_copy(k, way).wait_send()
            g_copy(k, way).wait_send()
            f_copy(k, way).wait_send()
        return carry

    lax.fori_loop(0, CHUNKS, drain, 0)


def on_device(grad_out, routes, gate_weights, gate_act, w_down, w_up):
    token_n, feat = grad_out.shape
    act, down, up = gate_act[0], w_down[0], w_up[0]
    hid_n = down.shape[0]
    hid = act.shape[1]
    tp_n = hid_n // hid
    msg = RING * SLOT
    half = token_n // 2
    dma = pltpu.SemaphoreType.DMA
    vmem = pl.BlockSpec(memory_space=pltpu.VMEM)
    hbm = pl.BlockSpec(memory_space=pl.ANY)
    return pl.pallas_call(
        on_core,
        out_shape=jax.ShapeDtypeStruct((token_n, feat), BF16),
        in_specs=[vmem, vmem, vmem, hbm, hbm, hbm],
        out_specs=vmem,
        scratch_shapes=[
            pltpu.VMEM(act.shape, BF16),
            pltpu.VMEM(down.shape, BF16),
            pltpu.VMEM(up.shape, BF16),
            pltpu.VMEM((CHUNKS, 2, msg, hid), BF16),
            pltpu.VMEM((RING, 32, token_n), F32),
            pltpu.VMEM((RING, 32, token_n), F32),
            pltpu.VMEM((RING, token_n, feat), BF16),
            pltpu.VMEM((CHUNKS, 2 * msg, RING * token_n), BF16),
            pltpu.VMEM((CHUNKS, 2, msg, feat), BF16),
            pltpu.VMEM((CHUNKS, 2, msg, feat), BF16),
            pltpu.VMEM((CHUNKS, tp_n, 2, msg, hid), BF16),
            pltpu.VMEM((CHUNKS, 2, msg, hid), BF16),
            pltpu.VMEM((CHUNKS, 2, msg, hid), BF16),
            pltpu.VMEM((CHUNKS, 2, 2, msg, hid), BF16),
            pltpu.VMEM((CHUNKS, tp_n, 2, msg, hid), BF16),
            pltpu.VMEM((CHUNKS, 2, msg, feat), BF16),
            pltpu.VMEM((CHUNKS, 2, msg, feat), BF16),
            pltpu.VMEM((RING, token_n, feat), F32),
            pltpu.VMEM((2, 2, 4, half, feat), BF16),
            pltpu.VMEM((2, 2, 4, half, feat), BF16),
            dma((3,)),
            dma((16,)), dma((16,)),
            dma((RING,)), dma((RING,)),
            dma((CHUNKS, 2)), dma((CHUNKS, 2)),
            dma((CHUNKS, 4)), dma((CHUNKS, 4)),
            dma((CHUNKS, 2)), dma((CHUNKS, 2)),
            dma((CHUNKS, 2)), dma((CHUNKS, 2)),
            dma((CHUNKS, 2)), dma((CHUNKS, 2)),
            dma((CHUNKS, 2)), dma((CHUNKS, 2)),
            dma((16,)), dma((16,)),
        ],
        compiler_params=pltpu.CompilerParams(
            collective_id=0, has_side_effects=True, vmem_limit_bytes=60 * 1024 * 1024
        ),
    )(grad_out, routes.T, gate_weights.T, act, down, up)


def solution(mesh):
    placed = (
        P("ep", "tp"),
        P("ep", None),
        P("ep", None),
        P("ep", None, "tp"),
        P("ep", None, "tp"),
        P("ep", "tp", None),
    )
    return jax.shard_map(
        on_device, mesh=mesh, in_specs=placed, out_specs=P("ep", "tp"), check_vma=False
    )
```

time: 372 us -> 131 us (0.35)
  waiting for transfers between devices: 169 us -> 0 us
  Pallas kernels: 0 us -> 127 us
  blocking collectives: 102 us -> 0 us
  local copies, waits for them, and re-layouts: 45.2 us -> 1.65 us
  starting transfers between devices: 15 us -> 0 us
  between operations: 13.5 us -> 0.01 us
  matrix products: 12.6 us -> 0 us
  other arithmetic: 10.6 us -> 0 us
    pallas_call x0 -> x1, Pallas kernels: none -> 127 us  [on_device(): pl.pallas_call(on_core, out_shape=jax.ShapeDtypeStruct((token_n, feat), B...]
    all_to_all x1 -> x0, blocking collectives: 102 us -> none  [on_device(): lax.all_to_all(placed, 'ep', split_axis=0, concat_axis=0, tiled=True)]
    all_to_all x1 -> x0, waiting for transfers between devices: 84.3 us -> none  [on_device(): lax.all_to_all(row_grad, 'ep', split_axis=0, concat_axis=0, tiled=True)]
    all_gather x1 -> x0, waiting for transfers between devices: 45.3 us -> none  [on_device(): lax.all_gather(up_grad, 'tp', axis=1, tiled=True)]
    reduce_scatter x1 -> x0, waiting for transfers between devices: 38.9 us -> none  [on_device(): lax.psum_scatter(partial_value.astype(jnp.bfloat16), 'tp', scatter_dimens...]
    all_to_all x1 -> x0, starting transfers between devices: 15 us -> none  [on_device(): lax.all_to_all(row_grad, 'ep', split_axis=0, concat_axis=0, tiled=True)]
    gather x2 -> x0, local copies, waits for them, and re-layouts: 12.7 us -> none  [the longest x1 7.67 us: on_device(): picked = returned.reshape(rows_n, -1)[position]]
    dot_general x2 -> x0, matrix products: 12.6 us -> none  [the longest x1 6.66 us: on_device(): lax.dot_general(lax.all_gather(up_grad, 'tp', axis=1, tiled=True), up_loc...]
  transfers between devices with their start and end apart: 3 -> 0, of which waited for: 3 -> 0; matrix products, arithmetic and copies ran while one was open for 0% -> 0% of each run, Pallas kernels for 0% -> 0%
where the time goes in v1:
time: 131 us; the launch traced here: 128 us
  Pallas kernels  127 us (97%)
  local copies, waits for them, and re-layouts  1.65 us (1%)
    pallas_call x1, Pallas kernels, on_device(): pl.pallas_call(on_core, out_shape=jax.ShapeDtypeStruct((token_n, feat), B...  127 us

profile of v1, /device:TPU:6, one launch (start us, length us, event | category | flops | bytes accessed | tf_op | source)
XLA Modules:
  0.0 128.3 jit_solution(5657592702556192230)
XLA Ops:
  0.0 126.6 %shard_map.64 = bf16[128,896]{1,0:T(8,128)(2,1)} custom-call(bf16[128,896]{1,0:T(8,128)(2,1)} %grad_ref.1, s32[8,128]{1,0:T(8,128)} %bitcast.8, f32[8,128]{1,0:T(8,128)} %bitcast.9, bf16[1280,256]{1,0:T(8,128)(2,1)} %bitcast.7, bf16[1024,896]{1,0:T(8,128)(2,1)} %bitcast.5, bf16[896,1024]{1,0:T(8,128)(2,1)} %bitcast.6), custom_call_target="tpu_custom_call" | custom-call | tf_op jit(solution)/shard_map/pallas_call | solution.py:400
  126.6 1.6 %copy.8 = bf16[128,896]{1,0:T(8,128)(2,1)} copy(bf16[128,896]{1,0:T(8,128)(2,1)} %shard_map.64) | data formatting | bytes 458752

commit v2 on v1

v2 whole, which is shorter than its diff:
```python
import functools

import jax
import jax.numpy as jnp
from jax import lax
from jax.experimental import pallas as pl
from jax.experimental.pallas import tpu as pltpu
from jax.sharding import PartitionSpec as P

MESH = pl.DeviceIdType.MESH
RING = 8
SLOT = 10
GROUPS = 4
HOPS = (2, 6, 3, 5, 4, 0, 1, 7)
HOP_CODE = sum(hop << (3 * i) for i, hop in enumerate(HOPS))
PIECES = 4
WAVES = ((0, 48, 0, 5), (48, 32, 4, 4))
NEAR = (0, 1, 7, 2, 6, 3, 5, 4)
PLACE = {offset: place for place, offset in enumerate(NEAR)}
COMBINE_LAG = 6
BF16 = jnp.bfloat16
F32 = jnp.float32
ABT = (((1,), (1,)), ((), ()))
ATB = (((0,), (0,)), ((), ()))


def hop_of(i):
    return (HOP_CODE >> (3 * i)) & 7


def on_core(
    grad_ref, ids_ref, gates_ref, act_hbm, down_hbm, up_hbm, out_ref,
    act, down, up, meta_out, meta, tokens, totals, sum_out, sum_in, waves,
    load_sem, a_send, a_recv, m_send, m_recv, b_send, b_recv, r_send, r_recv,
    p_send, p_recv, g_send, g_recv, f_send, f_recv, y_send, y_recv, s_send, s_recv,
):
    token_n, feat = grad_ref.shape
    piece = token_n // PIECES
    ep, tp = lax.axis_index("ep"), lax.axis_index("tp")
    tp_n = lax.axis_size("tp")
    core = lax.rem(ep, 2)
    y = lax.rem(ep // 2, RING)
    z = ep // (2 * RING)
    a = z * (1 - core) + y * core
    b = y * (1 - core) + z * core

    def device(a_at, b_at, role, core_at):
        return (a_at * (RING - (RING - 1) * role) + b_at * (1 + (RING - 1) * role)) * 2 + core_at

    def ring(value):
        return lax.rem(value + 2 * RING, RING)

    right, left = lax.rem(tp + 1, tp_n), lax.rem(tp + tp_n - 1, tp_n)
    across = lax.rem(tp + 2, tp_n)

    barrier = pltpu.get_barrier_semaphore()
    for other in range(2):
        for step in range(RING):
            for z_at, y_at in ((ring(z + step), y), (z, ring(y + step)))[: 1 if step == 0 else 2]:
                peer = (z_at * RING + y_at) * 2 + lax.rem(core + other, 2)
                if step or other:
                    pl.semaphore_signal(barrier, inc=1, device_id=(peer, tp), device_id_type=MESH)
    for peer in (right, left):
        pl.semaphore_signal(barrier, inc=1, device_id=(ep, peer), device_id_type=MESH)

    loads = [
        pltpu.make_async_copy(src, dst, load_sem.at[i])
        for i, (src, dst) in enumerate(((act_hbm, act), (down_hbm, down), (up_hbm, up)))
    ]
    for load in loads:
        load.start()

    def remote(src, dst, send, recv, to):
        return pltpu.make_async_remote_copy(
            src_ref=src, dst_ref=dst, send_sem=send, recv_sem=recv, device_id=to, device_id_type=MESH
        )

    def arrival(ref, sem):
        pltpu.make_async_copy(ref, ref, sem).wait()

    shape = (token_n, token_n)
    row = lax.broadcasted_iota(jnp.int32, shape, 0)
    chunk_of, core_of = (row >> 1) & 7, row & 1
    a_of = (row // 16 + a) & 7
    b_of = (hop_of(chunk_of) + b) & 7
    expert = a_of * (16 - 14 * core) + b_of * (2 + 14 * core) + core_of
    named = jnp.zeros(shape, F32)
    weight = jnp.zeros(shape, F32)
    for k in range(ids_ref.shape[0]):
        hit = expert == ids_ref[k : k + 1, :]
        named = jnp.where(hit, 1.0, named)
        weight = jnp.where(hit, gates_ref[k : k + 1, :], weight)
    before = (row < lax.broadcasted_iota(jnp.int32, shape, 1)).astype(BF16)
    rank = jnp.dot(named.astype(BF16), before, preferred_element_type=F32)
    slot = jnp.where(named > 0.0, rank, -1000.0)
    for m in range(RING):
        meta_out[m, 0:16, :] = slot[m * 16 : (m + 1) * 16, :]
        meta_out[m, 16:32, :] = weight[m * 16 : (m + 1) * 16, :]
    meta[0] = meta_out[0]
    tokens[0] = grad_ref[...]
    totals[...] = jnp.zeros(totals.shape, F32)

    pl.semaphore_wait(barrier, 4 * (RING - 1) + 1 + 2)

    a_next = (device(ring(a + 1), b, core, core), device(ring(a - 1), b, core, core))

    def steps_of(way, p):
        return 4 if (p < PIECES // 2) == (way == 0) else 3

    turns = [
        (way, (i + way * PIECES // 2) % PIECES) for i in range(PIECES) for way in range(2)
    ]

    def spread(way, p, s):
        rows = pl.ds(p * piece, piece)
        src_off, dst_off = ((RING - s) % RING, RING - 1 - s) if way == 0 else (s, s + 1)
        src = grad_ref.at[rows] if s == 0 else tokens.at[PLACE[src_off], rows]
        at = (way * PIECES + p) * 4 + s
        return remote(
            src, tokens.at[PLACE[dst_off], rows], a_send.at[at], a_recv.at[at], (a_next[way], tp)
        )

    for way, p in turns:
        spread(way, p, 0).start()
    metas = [
        remote(
            meta_out.at[m], meta.at[PLACE[RING - m]], m_send.at[m], m_recv.at[RING - m],
            (device(ring(a + m), b, core, core), tp),
        )
        for m in range(1, RING)
    ]
    for copy in metas:
        copy.start()

    act_n = act.shape[0]

    def order_act(w):
        row0, rows, _, _ = WAVES[w]
        wide_shape = (4 * rows, 128)
        row = lax.broadcasted_iota(jnp.int32, wide_shape, 0)
        lane = lax.broadcasted_iota(jnp.int32, wide_shape, 1)
        later = row >= 2 * rows
        inner = jnp.where(later, row - 2 * rows, row)
        from_one = inner >= rows
        inner = jnp.where(from_one, inner - rows, inner) + row0
        offset = jnp.full(wide_shape, NEAR[0], jnp.int32)
        in_slot = inner
        for place in range(1, RING):
            past = inner >= place * SLOT
            offset = jnp.where(past, NEAR[place], offset)
            in_slot = jnp.where(past, inner - place * SLOT, in_slot)
        base = in_slot + jnp.where(
            from_one,
            ((offset + y) & 7) * (2 * SLOT) + SLOT,
            ((offset + z) & 7) * (2 * SLOT * RING),
        )

        def order(i, carry):
            hop = jnp.where(later, hop_of(2 * i + 1), hop_of(2 * i))
            natural = base + jnp.where(
                from_one,
                ((z - hop) & 7) * (2 * SLOT * RING),
                ((y - hop) & 7) * (2 * SLOT),
            )
            pick = jnp.concatenate(
                [(lane + j * 128 == natural).astype(F32).astype(BF16) for j in range(act_n // 128)],
                axis=1,
            )
            got = jnp.dot(pick, act[...], preferred_element_type=F32).astype(BF16)
            ordered = waves[w]["act"]
            ordered[i] = got.reshape(ordered.shape[1:])
            return carry

        return order

    order = [order_act(w) for w in range(2)]

    def gather(w, i):
        row0, rows, place0, places = WAVES[w]
        wave = waves[w]
        msg_row = lax.broadcasted_iota(jnp.int32, (rows, token_n), 0).astype(F32) + float(row0)
        gates = []
        for n in range(4):
            at_row = 4 * i + n
            gate = jnp.zeros((rows, token_n), F32)
            for p in range(places):
                place = place0 + p
                at = meta[place, pl.ds(at_row, 1), :] + float(place * SLOT)
                hit = msg_row == at
                gate = jnp.where(hit, meta[place, pl.ds(16 + at_row, 1), :], gate)
                wave["picks"][i, n * rows : (n + 1) * rows, p * token_n : (p + 1) * token_n] = (
                    jnp.where(hit, 1.0, 0.0).astype(BF16)
                )
            gates.append(jnp.sum(gate, axis=1, keepdims=True))
        source = tokens[place0 : place0 + places].reshape(places * token_n, feat)
        value = jnp.dot(wave["picks"][i], source, preferred_element_type=F32)
        for n in range(4):
            wave["to_expert"][i, n // 2, n % 2] = (
                value[n * rows : (n + 1) * rows] * gates[n]
            ).astype(BF16)
        g = w * GROUPS + i
        for n in range(4):
            kk, c = n // 2, n % 2
            hop = hop_of(2 * i + kk)
            here = jnp.logical_and(hop == 0, core == c)
            src, dst = wave["to_expert"].at[i, kk, c], wave["routed"].at[i, kk, core]

            @pl.when(here)
            def _():
                pltpu.make_async_copy(src, dst, b_recv.at[g, kk, core]).start()

            @pl.when(jnp.logical_not(here))
            def _():
                remote(
                    src, dst, b_send.at[g, kk, c], b_recv.at[g, kk, core],
                    (device(a, ring(b + hop), core, c), tp),
                ).start()

    def spread_step(s):
        for way, p in turns:
            if s < steps_of(way, p):
                spread(way, p, s - 1).wait_recv()
                spread(way, p, s).start()

    def early(i, carry):
        gather(0, i)
        return carry

    loads[0].wait()
    lax.fori_loop(0, 2, order[0], 0)
    spread_step(1)
    lax.fori_loop(2, GROUPS, order[0], 0)
    spread_step(2)
    for m in range(1, RING):
        metas[m - 1].wait_recv()
    lax.fori_loop(0, 2, early, 0)
    spread_step(3)
    lax.fori_loop(2, GROUPS, early, 0)
    loads[1].wait()
    loads[2].wait()

    def r_copy(w, i, n):
        hidden, relay, arrived = waves[w]["hidden"], waves[w]["relay"], waves[w]["arrived"]
        src, dst, to = (
            (hidden.at[i, across, 0], relay.at[i, 0], right),
            (hidden.at[i, right, 1], arrived.at[i, 0, 1], right),
            (hidden.at[i, across, 1], relay.at[i, 1], left),
            (hidden.at[i, left, 0], arrived.at[i, 1, 0], left),
        )[n]
        g = w * GROUPS + i
        return remote(src, dst, r_send.at[g, n], r_recv.at[g, n], (ep, to))

    def p_copy(w, i, way):
        arrived = waves[w]["arrived"]
        dst, to = ((arrived.at[i, 0, 0], right), (arrived.at[i, 1, 1], left))[way]
        g = w * GROUPS + i
        return remote(
            waves[w]["passed"].at[i, way], dst, p_send.at[g, way], p_recv.at[g, way], (ep, to)
        )

    def g_copy(w, i, way):
        part = waves[w]["wide"].at[i, tp]
        g = w * GROUPS + i
        return remote(part, part, g_send.at[g, way], g_recv.at[g, way], (ep, (right, left)[way]))

    def f_copy(w, i, way):
        part = waves[w]["wide"].at[i, (left, right)[way], way]
        g = w * GROUPS + i
        return remote(part, part, f_send.at[g, way], f_recv.at[g, way], (ep, (right, left)[way]))

    def project_down(w, i):
        wave, rows = waves[w], WAVES[w][1]
        for kk in range(2):
            for c in range(2):
                arrival(wave["routed"].at[i, kk, c], b_recv.at[w * GROUPS + i, kk, c])
        got = wave["routed"][i].reshape(4 * rows, feat)
        hidden = wave["hidden"]
        part = hidden.shape[-1]
        for q in range(hidden.shape[1]):
            value = lax.dot_general(
                got, down[q * part : (q + 1) * part, :], ABT, preferred_element_type=F32
            )
            hidden[i, q] = value.astype(BF16).reshape(2, 2 * rows, part)
        for n in (0, 2, 1, 3):
            r_copy(w, i, n).start()

    def pass_on(w, i):
        wave = waves[w]
        for way, to in ((0, right), (1, left)):
            r_copy(w, i, way * 2).wait_recv()
            wave["passed"][i, way] = (
                wave["hidden"][i, to, way].astype(F32) + wave["relay"][i, way].astype(F32)
            ).astype(BF16)
            p_copy(w, i, way).start()

    def finish_hidden(w, i):
        wave = waves[w]
        r_copy(w, i, 1).wait_recv()
        r_copy(w, i, 3).wait_recv()
        p_copy(w, i, 0).wait_recv()
        p_copy(w, i, 1).wait_recv()
        value = wave["hidden"][i, tp].astype(F32) + (
            wave["arrived"][i, 0].astype(F32) + wave["arrived"][i, 1].astype(F32)
        )
        wave["wide"][i, tp] = (value * wave["act"][i].astype(F32)).astype(BF16)
        for way in range(2):
            g_copy(w, i, way).start()

    def hand_over(w, i):
        for way in range(2):
            arrival(waves[w]["wide"].at[i, (left, right)[way]], g_recv.at[w * GROUPS + i, way])
            f_copy(w, i, way).start()

    def project_up(w, i):
        wave, rows = waves[w], WAVES[w][1]
        wide = wave["wide"]
        g = w * GROUPS + i
        for way in range(2):
            arrival(wide.at[i, across, way], f_recv.at[g, way])
        part = wide.shape[-1]
        got = jnp.concatenate(
            [wide[i, q].reshape(4 * rows, part) for q in range(wide.shape[1])], axis=1
        )
        value = lax.dot_general(got, up[...], ABT, preferred_element_type=F32).astype(BF16)
        wave["row_grad"][i] = value.reshape(2, 2, rows, feat)
        for n in range(4):
            kk, c = n // 2, n % 2
            hop = hop_of(2 * i + kk)
            here = jnp.logical_and(hop == 0, core == c)
            to = device(z, ring(y - hop), 0, 0) if c == 0 else device(y, ring(z - hop), 1, 1)
            src, dst = wave["row_grad"].at[i, kk, c], wave["returned"].at[i, kk, core]

            @pl.when(here)
            def _():
                pltpu.make_async_copy(src, dst, y_recv.at[g, kk, core]).start()

            @pl.when(jnp.logical_not(here))
            def _():
                remote(
                    src, dst, y_send.at[g, kk, c], y_recv.at[g, kk, core], (to, tp)
                ).start()

    def combine(w, i):
        _, rows, place0, places = WAVES[w]
        wave = waves[w]
        for kk in range(2):
            for c in range(2):
                arrival(wave["returned"].at[i, kk, c], y_recv.at[w * GROUPS + i, kk, c])
        got = wave["returned"][i].reshape(4 * rows, feat)
        value = lax.dot_general(wave["picks"][i], got, ATB, preferred_element_type=F32)
        totals[place0 : place0 + places] += value.reshape(places, token_n, feat)

    stages = (
        (project_down, 0),
        (pass_on, 1),
        (finish_hidden, 2),
        (hand_over, 3),
        (project_up, 4),
        (combine, COMBINE_LAG),
    )

    def turn(t, carry):
        for stage, lag in stages:
            for w in range(2):
                first = lag + w * GROUPS

                @pl.when(jnp.logical_and(t >= first, t < first + GROUPS))
                def _():
                    stage(w, t - first)

            if lag == 0:

                @pl.when(t == 0)
                def _():
                    for way, p in turns:
                        spread(way, p, steps_of(way, p) - 1).wait_recv()

                @pl.when(t < GROUPS)
                def _():
                    gather(1, t)
                    order[1](t, 0)

        return carry

    lax.fori_loop(0, 2 * GROUPS + COMBINE_LAG, turn, 0)

    def chain_of(way, p):
        chain = (4, 3, 2, 1) if way == 0 else (4, 5, 6, 7)
        return chain[4 - steps_of(way, p) :]

    def sum_copy(way, p, s):
        at = (way * PIECES + p) * 4 + s
        return remote(
            sum_out.at[way, p, s], sum_in.at[way, p, s], s_send.at[at], s_recv.at[at],
            (a_next[way], tp),
        )

    for s in range(4):
        for way, p in turns:
            chain = chain_of(way, p)
            if s < len(chain):
                value = totals[PLACE[chain[s]], p * piece : (p + 1) * piece, :]
                if s:
                    sum_copy(way, p, s - 1).wait_recv()
                    value = value + sum_in[way, p, s - 1].astype(F32)
                sum_out[way, p, s] = value.astype(BF16)
                sum_copy(way, p, s).start()
    for i in range(PIECES):
        p = (i + PIECES // 2) % PIECES
        value = totals[0, p * piece : (p + 1) * piece, :]
        for way in range(2):
            last = steps_of(way, p) - 1
            sum_copy(way, p, last).wait_recv()
            value = value + sum_in[way, p, last].astype(F32)
        out_ref[p * piece : (p + 1) * piece, :] = value.astype(BF16)

    for copy in metas:
        copy.wait_send()
    for way, p in turns:
        for s in range(steps_of(way, p)):
            spread(way, p, s).wait_send()
            sum_copy(way, p, s).wait_send()

    def drain(i, carry):
        for w in range(2):
            g = w * GROUPS + i
            for kk in range(2):
                hop = hop_of(2 * i + kk)
                for c in range(2):

                    @pl.when(jnp.logical_not(jnp.logical_and(hop == 0, core == c)))
                    def _():
                        arrival(waves[w]["to_expert"].at[i, kk, c], b_send.at[g, kk, c])
                        arrival(waves[w]["row_grad"].at[i, kk, c], y_send.at[g, kk, c])

            for n in range(4):
                r_copy(w, i, n).wait_send()
            for way in range(2):
                p_copy(w, i, way).wait_send()
                g_copy(w, i, way).wait_send()
                f_copy(w, i, way).wait_send()
        return carry

    lax.fori_loop(0, GROUPS, drain, 0)


def scratch_of(wave, token_n, feat, hid, tp_n):
    _, rows, _, places = wave
    shapes = {
        "act": (2, 2 * rows, hid),
        "picks": (4 * rows, places * token_n),
        "to_expert": (2, 2, rows, feat),
        "routed": (2, 2, rows, feat),
        "hidden": (tp_n, 2, 2 * rows, hid),
        "relay": (2, 2 * rows, hid),
        "passed": (2, 2 * rows, hid),
        "arrived": (2, 2, 2 * rows, hid),
        "wide": (tp_n, 2, 2 * rows, hid),
        "row_grad": (2, 2, rows, feat),
        "returned": (2, 2, rows, feat),
    }
    return {name: pltpu.VMEM((GROUPS,) + shape, BF16) for name, shape in shapes.items()}


def on_device(grad_out, routes, gate_weights, gate_act, w_down, w_up):
    token_n, feat = grad_out.shape
    act, down, up = gate_act[0], w_down[0], w_up[0]
    hid_n = down.shape[0]
    hid = act.shape[1]
    tp_n = hid_n // hid
    piece = token_n // PIECES
    chunks = 2 * GROUPS
    dma = pltpu.SemaphoreType.DMA
    vmem = pl.BlockSpec(memory_space=pltpu.VMEM)
    hbm = pl.BlockSpec(memory_space=pl.ANY)
    return pl.pallas_call(
        on_core,
        out_shape=jax.ShapeDtypeStruct((token_n, feat), BF16),
        in_specs=[vmem, vmem, vmem, hbm, hbm, hbm],
        out_specs=vmem,
        scratch_shapes=[
            pltpu.VMEM(act.shape, BF16),
            pltpu.VMEM(down.shape, BF16),
            pltpu.VMEM(up.shape, BF16),
            pltpu.VMEM((RING, 32, token_n), F32),
            pltpu.VMEM((RING, 32, token_n), F32),
            pltpu.VMEM((RING, token_n, feat), BF16),
            pltpu.VMEM((RING, token_n, feat), F32),
            pltpu.VMEM((2, PIECES, 4, piece, feat), BF16),
            pltpu.VMEM((2, PIECES, 4, piece, feat), BF16),
            [scratch_of(wave, token_n, feat, hid, tp_n) for wave in WAVES],
            dma((3,)),
            dma((8 * PIECES,)), dma((8 * PIECES,)),
            dma((RING,)), dma((RING,)),
            dma((chunks, 2, 2)), dma((chunks, 2, 2)),
            dma((chunks, 4)), dma((chunks, 4)),
            dma((chunks, 2)), dma((chunks, 2)),
            dma((chunks, 2)), dma((chunks, 2)),
            dma((chunks, 2)), dma((chunks, 2)),
            dma((chunks, 2, 2)), dma((chunks, 2, 2)),
            dma((8 * PIECES,)), dma((8 * PIECES,)),
        ],
        compiler_params=pltpu.CompilerParams(
            collective_id=0, has_side_effects=True, vmem_limit_bytes=60 * 1024 * 1024
        ),
    )(grad_out, routes.T, gate_weights.T, act, down, up)


def solution(mesh):
    placed = (
        P("ep", "tp"),
        P("ep", None),
        P("ep", None),
        P("ep", None, "tp"),
        P("ep", None, "tp"),
        P("ep", "tp", None),
    )
    return jax.shard_map(
        on_device, mesh=mesh, in_specs=placed, out_specs=P("ep", "tp"), check_vma=False
    )
```

time: 131 us -> 115 us (0.88)
  Pallas kernels: 127 us -> 112 us
    pallas_call x1, Pallas kernels: 127 us -> 112 us  [on_device(): pl.pallas_call(on_core, out_shape=jax.ShapeDtypeStruct((token_n, feat), B...]
where the time goes in v2:
time: 115 us; the launch traced here: 113 us
  Pallas kernels  112 us (97%)
  local copies, waits for them, and re-layouts  1.65 us (1%)
    pallas_call x1, Pallas kernels, on_device(): pl.pallas_call(on_core, out_shape=jax.ShapeDtypeStruct((token_n, feat), B...  112 us

profile of v2, /device:TPU:6, one launch (start us, length us, event | category | flops | bytes accessed | tf_op | source)
XLA Modules:
  0.0 113.4 jit_solution(626114564188338530)
XLA Ops:
  0.0 111.8 %shard_map.64 = bf16[128,896]{1,0:T(8,128)(2,1)} custom-call(bf16[128,896]{1,0:T(8,128)(2,1)} %grad_ref.1, s32[8,128]{1,0:T(8,128)} %bitcast.8, f32[8,128]{1,0:T(8,128)} %bitcast.9, bf16[1280,256]{1,0:T(8,128)(2,1)} %bitcast.7, bf16[1024,896]{1,0:T(8,128)(2,1)} %bitcast.5, bf16[896,1024]{1,0:T(8,128)(2,1)} %bitcast.6), custom_call_target="tpu_custom_call" | custom-call | tf_op jit(solution)/shard_map/pallas_call | solution.py:476
  111.8 1.6 %copy.8 = bf16[128,896]{1,0:T(8,128)(2,1)} copy(bf16[128,896]{1,0:T(8,128)(2,1)} %shard_map.64) | data formatting | bytes 458752

commit v3 on v2

--- a/solution.py
+++ b/solution.py
@@ -11,8 +11,9 @@
 RING = 8
 SLOT = 10
 GROUPS = 4
-HOPS = (2, 6, 3, 5, 4, 0, 1, 7)
+HOPS = (1, 7, 3, 5, 0, 4, 2, 6)
 HOP_CODE = sum(hop << (3 * i) for i, hop in enumerate(HOPS))
+EARLY = 2
 PIECES = 4
 WAVES = ((0, 48, 0, 5), (48, 32, 4, 4))
 NEAR = (0, 1, 7, 2, 6, 3, 5, 4)
@@ -24,8 +25,16 @@
 ATB = (((0,), (0,)), ((), ()))
 
 
-def hop_of(i):
+def hop_at(i):
     return (HOP_CODE >> (3 * i)) & 7
+
+
+def pair_of(w, i):
+    return i if w == 0 else lax.rem(i + 1, GROUPS)
+
+
+def hop_of(w, i, kk):
+    return hop_at(2 * pair_of(w, i) + kk)
 
 
 def on_core(
@@ -78,11 +87,33 @@
     def arrival(ref, sem):
         pltpu.make_async_copy(ref, ref, sem).wait()
 
+    pl.semaphore_wait(barrier, 4 * (RING - 1) + 1 + 2)
+
+    a_next = (device(ring(a + 1), b, core, core), device(ring(a - 1), b, core, core))
+
+    def steps_of(way, p):
+        return 4 if (p < PIECES // 2) == (way == 0) else 3
+
+    turns = [
+        (way, (i + way * PIECES // 2) % PIECES) for i in range(PIECES) for way in range(2)
+    ]
+
+    def spread(way, p, s):
+        rows = pl.ds(p * piece, piece)
+        src_off, dst_off = ((RING - s) % RING, RING - 1 - s) if way == 0 else (s, s + 1)
+        src = grad_ref.at[rows] if s == 0 else tokens.at[PLACE[src_off], rows]
+        at = (way * PIECES + p) * 4 + s
+        return remote(
+            src, tokens.at[PLACE[dst_off], rows], a_send.at[at], a_recv.at[at], (a_next[way], tp)
+        )
+
+    for way, p in turns:
+        spread(way, p, 0).start()
     shape = (token_n, token_n)
     row = lax.broadcasted_iota(jnp.int32, shape, 0)
     chunk_of, core_of = (row >> 1) & 7, row & 1
     a_of = (row // 16 + a) & 7
-    b_of = (hop_of(chunk_of) + b) & 7
+    b_of = (hop_at(chunk_of) + b) & 7
     expert = a_of * (16 - 14 * core) + b_of * (2 + 14 * core) + core_of
     named = jnp.zeros(shape, F32)
     weight = jnp.zeros(shape, F32)
@@ -97,31 +128,6 @@
         meta_out[m, 0:16, :] = slot[m * 16 : (m + 1) * 16, :]
         meta_out[m, 16:32, :] = weight[m * 16 : (m + 1) * 16, :]
     meta[0] = meta_out[0]
-    tokens[0] = grad_ref[...]
-    totals[...] = jnp.zeros(totals.shape, F32)
-
-    pl.semaphore_wait(barrier, 4 * (RING - 1) + 1 + 2)
-
-    a_next = (device(ring(a + 1), b, core, core), device(ring(a - 1), b, core, core))
-
-    def steps_of(way, p):
-        return 4 if (p < PIECES // 2) == (way == 0) else 3
-
-    turns = [
-        (way, (i + way * PIECES // 2) % PIECES) for i in range(PIECES) for way in range(2)
-    ]
-
-    def spread(way, p, s):
-        rows = pl.ds(p * piece, piece)
-        src_off, dst_off = ((RING - s) % RING, RING - 1 - s) if way == 0 else (s, s + 1)
-        src = grad_ref.at[rows] if s == 0 else tokens.at[PLACE[src_off], rows]
-        at = (way * PIECES + p) * 4 + s
-        return remote(
-            src, tokens.at[PLACE[dst_off], rows], a_send.at[at], a_recv.at[at], (a_next[way], tp)
-        )
-
-    for way, p in turns:
-        spread(way, p, 0).start()
     metas = [
         remote(
             meta_out.at[m], meta.at[PLACE[RING - m]], m_send.at[m], m_recv.at[RING - m],
@@ -156,7 +162,7 @@
         )
 
         def order(i, carry):
-            hop = jnp.where(later, hop_of(2 * i + 1), hop_of(2 * i))
+            hop = jnp.where(later, hop_of(w, i, 1), hop_of(w, i, 0))
             natural = base + jnp.where(
                 from_one,
                 ((z - hop) & 7) * (2 * SLOT * RING),
@@ -181,7 +187,7 @@
         msg_row = lax.broadcasted_iota(jnp.int32, (rows, token_n), 0).astype(F32) + float(row0)
         gates = []
         for n in range(4):
-            at_row = 4 * i + n
+            at_row = 4 * pair_of(w, i) + n
             gate = jnp.zeros((rows, token_n), F32)
             for p in range(places):
                 place = place0 + p
@@ -201,7 +207,7 @@
         g = w * GROUPS + i
         for n in range(4):
             kk, c = n // 2, n % 2
-            hop = hop_of(2 * i + kk)
+            hop = hop_of(w, i, kk)
             here = jnp.logical_and(hop == 0, core == c)
             src, dst = wave["to_expert"].at[i, kk, c], wave["routed"].at[i, kk, core]
 
@@ -226,16 +232,17 @@
         gather(0, i)
         return carry
 
+    tokens[0] = grad_ref[...]
+    totals[...] = jnp.zeros(totals.shape, F32)
     loads[0].wait()
-    lax.fori_loop(0, 2, order[0], 0)
+    lax.fori_loop(0, 1, order[0], 0)
     spread_step(1)
-    lax.fori_loop(2, GROUPS, order[0], 0)
+    lax.fori_loop(1, GROUPS, order[0], 0)
     spread_step(2)
     for m in range(1, RING):
         metas[m - 1].wait_recv()
-    lax.fori_loop(0, 2, early, 0)
+    lax.fori_loop(0, EARLY, early, 0)
     spread_step(3)
-    lax.fori_loop(2, GROUPS, early, 0)
     loads[1].wait()
     loads[2].wait()
 
@@ -325,7 +332,7 @@
         wave["row_grad"][i] = value.reshape(2, 2, rows, feat)
         for n in range(4):
             kk, c = n // 2, n % 2
-            hop = hop_of(2 * i + kk)
+            hop = hop_of(w, i, kk)
             here = jnp.logical_and(hop == 0, core == c)
             to = device(z, ring(y - hop), 0, 0) if c == 0 else device(y, ring(z - hop), 1, 1)
             src, dst = wave["row_grad"].at[i, kk, c], wave["returned"].at[i, kk, core]
@@ -359,31 +366,6 @@
         (combine, COMBINE_LAG),
     )
 
-    def turn(t, carry):
-        for stage, lag in stages:
-            for w in range(2):
-                first = lag + w * GROUPS
-
-                @pl.when(jnp.logical_and(t >= first, t < first + GROUPS))
-                def _():
-                    stage(w, t - first)
-
-            if lag == 0:
-
-                @pl.when(t == 0)
-                def _():
-                    for way, p in turns:
-                        spread(way, p, steps_of(way, p) - 1).wait_recv()
-
-                @pl.when(t < GROUPS)
-                def _():
-                    gather(1, t)
-                    order[1](t, 0)
-
-        return carry
-
-    lax.fori_loop(0, 2 * GROUPS + COMBINE_LAG, turn, 0)
-
     def chain_of(way, p):
         chain = (4, 3, 2, 1) if way == 0 else (4, 5, 6, 7)
         return chain[4 - steps_of(way, p) :]
@@ -395,16 +377,65 @@
             (a_next[way], tp),
         )
 
-    for s in range(4):
+    def add_on(offsets):
         for way, p in turns:
-            chain = chain_of(way, p)
-            if s < len(chain):
-                value = totals[PLACE[chain[s]], p * piece : (p + 1) * piece, :]
-                if s:
-                    sum_copy(way, p, s - 1).wait_recv()
-                    value = value + sum_in[way, p, s - 1].astype(F32)
-                sum_out[way, p, s] = value.astype(BF16)
-                sum_copy(way, p, s).start()
+            for s, offset in enumerate(chain_of(way, p)):
+                if offset in offsets:
+                    value = totals[PLACE[offset], p * piece : (p + 1) * piece, :]
+                    if s:
+                        sum_copy(way, p, s - 1).wait_recv()
+                        value = value + sum_in[way, p, s - 1].astype(F32)
+                    sum_out[way, p, s] = value.astype(BF16)
+                    sum_copy(way, p, s).start()
+
+    last = EARLY + GROUPS
+
+    def turn(t, carry):
+        for stage, lag in stages:
+            g = t - lag
+
+            @pl.when(jnp.logical_and(g >= 0, g < EARLY))
+            def _():
+                stage(0, g)
+
+            @pl.when(jnp.logical_and(g >= EARLY, g < last))
+            def _():
+                stage(1, g - EARLY)
+
+            @pl.when(jnp.logical_and(g >= last, g < 2 * GROUPS))
+            def _():
+                stage(0, g - GROUPS)
+
+            if lag == 0:
+
+                @pl.when(t == 0)
+                def _():
+                    for way, p in turns:
+                        spread(way, p, steps_of(way, p) - 1).wait_recv()
+
+                @pl.when(t < GROUPS)
+                def _():
+                    gather(1, t)
+                    order[1](t, 0)
+
+                @pl.when(jnp.logical_and(t >= GROUPS, t < 2 * GROUPS - EARLY))
+                def _():
+                    gather(0, t - GROUPS + EARLY)
+
+        @pl.when(t == last - 1 + COMBINE_LAG)
+        def _():
+            add_on((4,))
+
+        @pl.when(t == last + COMBINE_LAG)
+        def _():
+            add_on((3, 5))
+
+        return carry
+
+    lax.fori_loop(0, 2 * GROUPS + COMBINE_LAG, turn, 0)
+    add_on((2, 6))
+    add_on((1, 7))
+
     for i in range(PIECES):
         p = (i + PIECES // 2) % PIECES
         value = totals[0, p * piece : (p + 1) * piece, :]
@@ -425,7 +456,7 @@
         for w in range(2):
             g = w * GROUPS + i
             for kk in range(2):
-                hop = hop_of(2 * i + kk)
+                hop = hop_of(w, i, kk)
                 for c in range(2):
 
                     @pl.when(jnp.logical_not(jnp.logical_and(hop == 0, core == c)))

time: 115 us -> 121 us (1.052); the launches traced: 113 us -> 121 us
  Pallas kernels: 112 us -> 119 us
    pallas_call x1, Pallas kernels: 112 us -> 119 us  [on_device(): pl.pallas_call(on_core, out_shape=jax.ShapeDtypeStruct((token_n, feat), B...]
where the time goes in v3:
time: 121 us
  Pallas kernels  119 us (98%)
  local copies, waits for them, and re-layouts  1.65 us (1%)
    pallas_call x1, Pallas kernels, on_device(): pl.pallas_call(on_core, out_shape=jax.ShapeDtypeStruct((token_n, feat), B...  119 us

profile of v3, /device:TPU:6, one launch (start us, length us, event | category | flops | bytes accessed | tf_op | source)
XLA Modules:
  0.0 121.1 jit_solution(6782979166332002384)
XLA Ops:
  0.0 119.5 %shard_map.64 = bf16[128,896]{1,0:T(8,128)(2,1)} custom-call(bf16[128,896]{1,0:T(8,128)(2,1)} %grad_ref.1, s32[8,128]{1,0:T(8,128)} %bitcast.8, f32[8,128]{1,0:T(8,128)} %bitcast.9, bf16[1280,256]{1,0:T(8,128)(2,1)} %bitcast.7, bf16[1024,896]{1,0:T(8,128)(2,1)} %bitcast.5, bf16[896,1024]{1,0:T(8,128)(2,1)} %bitcast.6), custom_call_target="tpu_custom_call" | custom-call | tf_op jit(solution)/shard_map/pallas_call | solution.py:507
  119.5 1.6 %copy.8 = bf16[128,896]{1,0:T(8,128)(2,1)} copy(bf16[128,896]{1,0:T(8,128)(2,1)} %shard_map.64) | data formatting | bytes 458752

commit v4 on v3

--- a/solution.py
+++ b/solution.py
@@ -11,7 +11,7 @@
 RING = 8
 SLOT = 10
 GROUPS = 4
-HOPS = (1, 7, 3, 5, 0, 4, 2, 6)
+HOPS = (1, 7, 0, 4, 3, 5, 2, 6)
 HOP_CODE = sum(hop << (3 * i) for i, hop in enumerate(HOPS))
 EARLY = 2
 PIECES = 4
@@ -30,7 +30,7 @@
 
 
 def pair_of(w, i):
-    return i if w == 0 else lax.rem(i + 1, GROUPS)
+    return i
 
 
 def hop_of(w, i, kk):

time: 121 us -> 113 us (0.934)
  Pallas kernels: 119 us -> 111 us
    pallas_call x1, Pallas kernels: 119 us -> 111 us  [on_device(): pl.pallas_call(on_core, out_shape=jax.ShapeDtypeStruct((token_n, feat), B...]
where the time goes in v4:
time: 113 us; the launch traced here: 112 us
  Pallas kernels  111 us (98%)
  local copies, waits for them, and re-layouts  1.65 us (1%)
    pallas_call x1, Pallas kernels, on_device(): pl.pallas_call(on_core, out_shape=jax.ShapeDtypeStruct((token_n, feat), B...  111 us

profile of v4, /device:TPU:6, one launch (start us, length us, event | category | flops | bytes accessed | tf_op | source)
XLA Modules:
  0.0 112.2 jit_solution(2324567965946141172)
XLA Ops:
  0.0 110.5 %shard_map.64 = bf16[128,896]{1,0:T(8,128)(2,1)} custom-call(bf16[128,896]{1,0:T(8,128)(2,1)} %grad_ref.1, s32[8,128]{1,0:T(8,128)} %bitcast.8, f32[8,128]{1,0:T(8,128)} %bitcast.9, bf16[1280,256]{1,0:T(8,128)(2,1)} %bitcast.7, bf16[1024,896]{1,0:T(8,128)(2,1)} %bitcast.5, bf16[896,1024]{1,0:T(8,128)(2,1)} %bitcast.6), custom_call_target="tpu_custom_call" | custom-call | tf_op jit(solution)/shard_map/pallas_call | solution.py:507
  110.6 1.6 %copy.8 = bf16[128,896]{1,0:T(8,128)(2,1)} copy(bf16[128,896]{1,0:T(8,128)(2,1)} %shard_map.64) | data formatting | bytes 458752

commit v5 on v4

--- a/solution.py
+++ b/solution.py
@@ -18,7 +18,7 @@
 WAVES = ((0, 48, 0, 5), (48, 32, 4, 4))
 NEAR = (0, 1, 7, 2, 6, 3, 5, 4)
 PLACE = {offset: place for place, offset in enumerate(NEAR)}
-COMBINE_LAG = 6
+COMBINE_LAG = 7
 BF16 = jnp.bfloat16
 F32 = jnp.float32
 ABT = (((1,), (1,)), ((), ()))

time: 113 us -> 113 us (level)
  no operation moved by 1% of the time
where the time goes in v5:
time: 113 us
  Pallas kernels  111 us (98%)
  local copies, waits for them, and re-layouts  1.65 us (1%)
    pallas_call x1, Pallas kernels, on_device(): pl.pallas_call(on_core, out_shape=jax.ShapeDtypeStruct((token_n, feat), B...  111 us

profile of v5, /device:TPU:6, one launch (start us, length us, event | category | flops | bytes accessed | tf_op | source)
XLA Modules:
  0.0 112.9 jit_solution(8812964109633701926)
XLA Ops:
  0.0 111.3 %shard_map.64 = bf16[128,896]{1,0:T(8,128)(2,1)} custom-call(bf16[128,896]{1,0:T(8,128)(2,1)} %grad_ref.1, s32[8,128]{1,0:T(8,128)} %bitcast.8, f32[8,128]{1,0:T(8,128)} %bitcast.9, bf16[1280,256]{1,0:T(8,128)(2,1)} %bitcast.7, bf16[1024,896]{1,0:T(8,128)(2,1)} %bitcast.5, bf16[896,1024]{1,0:T(8,128)(2,1)} %bitcast.6), custom_call_target="tpu_custom_call" | custom-call | tf_op jit(solution)/shard_map/pallas_call | solution.py:507
  111.3 1.6 %copy.8 = bf16[128,896]{1,0:T(8,128)(2,1)} copy(bf16[128,896]{1,0:T(8,128)(2,1)} %shard_map.64) | data formatting | bytes 458752
